TPU v7x, 256 devices: a whole 4x4x8 slice. The times are simulated.
256 devices in a mesh: seq: 16 (over z, core), fsdp: 16 (over x, y).
Axes of the slice: x: 4, y: 4, z: 8, core: 2. Of those that a mesh axis runs over, the one named last changes fastest.
Arguments:
- inputs: bfloat16 [16, 2048, 2304], P('fsdp', 'seq'), may hold values from -6 to 6
- queries: bfloat16 [16, 2048, 2048], P('fsdp', 'seq'), may hold values from -96 to 96
- w_kv: bfloat16 [2304, 2048], P('fsdp'), may hold values from -0.125 to 0.125
- doc_lengths: int32 [16, 8], P('fsdp'), may hold values from 1 to 1536, 2048 in all within a row
- grad_out: bfloat16 [16, 2048, 2048], P('fsdp', 'seq'), may hold values from -6 to 6
Outputs:
- attn_out: bfloat16 [16, 2048, 2048], P('fsdp', 'seq')
- grad_inputs: bfloat16 [16, 2048, 2304], P('fsdp', 'seq')
- grad_weights: float32 [2304, 2048], P('fsdp', 'seq')
Inputs may be any that keep to these rules, and one draw needn't show every extreme that they name: `doc_lengths`: each row lists the lengths of the 8 documents packed in order into one sequence; a row sums to 2048 and its longest document has 1536 tokens.
All inputs are finite; a program needn't handle non-finite values.
Results may differ from a plain program's by a relative error of at most 0.03.
Values may be sent and summed in bfloat16 or wider, within the bound.
A program may use at most 128 MiB of HBM per device.

v0:
```python
import jax
import jax.numpy as jnp
from jax import lax
from jax.sharding import PartitionSpec as P

QH = 16
KVH = 8
HD = 128
WIN = 1024
G = 2
SOFT_CAP = 50.0
QUERY_SCALE = 1.0 / 12.0
ROPE_BASE = 10000.0


def from_behind(value, axis, steps):
    count = lax.axis_size(axis)
    first, last = (max(0, -steps), min(count, count - steps))
    return lax.ppermute(value, axis, [(source, source + steps) for source in range(first, last)])


def doc_layout(lengths, places):
    doc_ends = jnp.cumsum(lengths)
    doc_ended = doc_ends[None, :] <= places[:, None]
    doc_index = jnp.sum(doc_ended.astype(jnp.int32), axis=1)
    before = jnp.sum(jnp.where(doc_ended, lengths[None, :], 0), axis=1)
    return (doc_index, places - before)


def rotate(values, places, direction):
    half_dim = values.shape[-1] // 2
    exponent = jnp.arange(half_dim, dtype=jnp.float32) * (2.0 / values.shape[-1])
    inverse_rate = jnp.power(ROPE_BASE, -exponent)
    angles = places.astype(jnp.float32)[:, None] * inverse_rate[None, :]
    cosine = jnp.cos(angles)[:, None, :]
    sine_part = direction * jnp.sin(angles)[:, None, :]
    first_half = values[..., :half_dim]
    second_half = values[..., half_dim:]
    return jnp.concatenate(
        [
            first_half * cosine - second_half * sine_part,
            second_half * cosine + first_half * sine_part,
        ],
        axis=-1,
    )


def attend(earlier, query_rows, cotangent, window, allowed):
    row_count = query_rows.shape[0]
    used_rows = (earlier + 1) * row_count
    half_kv = KVH * HD
    pair_width = 2 * G * HD

    def one_pair(pair_index, state_now):
        out_acc, key_acc, value_acc = state_now
        q_part = lax.dynamic_slice_in_dim(
            query_rows, pair_index * pair_width, pair_width, 1
        ).reshape(row_count, 2, G, HD)
        d_part = lax.dynamic_slice_in_dim(
            cotangent, pair_index * pair_width, pair_width, 1
        ).reshape(row_count, 2, G, HD)
        k_part = lax.dynamic_slice_in_dim(window, pair_index * 2 * HD, 2 * HD, 1).reshape(
            used_rows, 2, HD
        )
        v_part = lax.dynamic_slice_in_dim(window, half_kv + pair_index * 2 * HD, 2 * HD, 1).reshape(
            used_rows, 2, HD
        )
        scores = (
            jnp.einsum("tkgd,nkd->kgtn", q_part, k_part, preferred_element_type=jnp.float32)
            * QUERY_SCALE
        )
        squashed = jnp.tanh(scores / SOFT_CAP)
        weights = jnp.where(allowed[None, None], jnp.exp(SOFT_CAP * squashed), 0.0)
        probs = weights / jnp.sum(weights, axis=-1, keepdims=True)
        rounded = probs.astype(jnp.bfloat16)
        attended = jnp.einsum(
            "kgtn,nkd->tkgd", rounded, v_part, preferred_element_type=jnp.float32
        ).astype(jnp.bfloat16)
        delta_row = jnp.einsum(
            "tkgd,tkgd->kgt", d_part, attended, preferred_element_type=jnp.float32
        )
        dprob = jnp.einsum("tkgd,nkd->kgtn", d_part, v_part, preferred_element_type=jnp.float32)
        dscore = (probs * (dprob - delta_row[..., None]) * (1.0 - squashed * squashed)).astype(
            jnp.bfloat16
        )
        key_grad = (
            jnp.einsum("kgtn,tkgd->nkd", dscore, q_part, preferred_element_type=jnp.float32)
            * QUERY_SCALE
        )
        value_grad = jnp.einsum(
            "kgtn,tkgd->nkd", rounded, d_part, preferred_element_type=jnp.float32
        )
        out_acc = lax.dynamic_update_slice_in_dim(
            out_acc, attended.reshape(row_count, pair_width), pair_index * pair_width, 1
        )
        key_acc = lax.dynamic_update_slice_in_dim(
            key_acc, key_grad.reshape(used_rows, 2 * HD), pair_index * 2 * HD, 1
        )
        value_acc = lax.dynamic_update_slice_in_dim(
            value_acc, value_grad.reshape(used_rows, 2 * HD), pair_index * 2 * HD, 1
        )
        return (out_acc, key_acc, value_acc)

    initial = (
        jnp.zeros((row_count, QH * HD), jnp.bfloat16),
        jnp.zeros((used_rows, half_kv), jnp.float32),
        jnp.zeros((used_rows, half_kv), jnp.float32),
    )
    out_rows, key_grads, value_grads = lax.fori_loop(0, KVH // 2, one_pair, initial)
    return (out_rows, key_grads, value_grads)


def on_device(inputs, queries, w_kv, doc_lengths, grad_out):
    tokens = inputs[0]
    query_rows = queries[0]
    cotangent = grad_out[0]
    lengths = doc_lengths[0]
    row_count = tokens.shape[0]
    seq_count = lax.axis_size("seq")
    shard_index = lax.axis_index("seq")
    reach_blocks = min((WIN + row_count - 2) // row_count, seq_count - 1)
    half_kv = KVH * HD
    weight_full = lax.all_gather(w_kv, "fsdp", axis=0, tiled=True)
    projected = jnp.dot(tokens, weight_full, preferred_element_type=jnp.float32)
    places = shard_index * row_count + jnp.arange(row_count, dtype=jnp.int32)
    doc_index, within = doc_layout(lengths, places)
    own_keys = rotate(projected[:, :half_kv].reshape(row_count, KVH, HD), within, 1.0).reshape(
        row_count, half_kv
    )
    own_block = jnp.concatenate([own_keys, projected[:, half_kv:]], axis=1).astype(jnp.bfloat16)
    received = [own_block]
    for offset in range(1, reach_blocks + 1):
        received.append(from_behind(own_block, "seq", offset))
    window = jnp.concatenate(received[::-1], axis=0)
    key_places = (shard_index - reach_blocks) * row_count + jnp.arange(
        (reach_blocks + 1) * row_count, dtype=jnp.int32
    )
    key_doc, ignored = doc_layout(lengths, key_places)
    distance = places[:, None] - key_places[None, :]
    allowed = (
        (key_places[None, :] >= 0)
        & (doc_index[:, None] == key_doc[None, :])
        & (distance >= 0)
        & (distance <= WIN - 1)
    )
    out_rows, key_grads, value_grads = attend(reach_blocks, query_rows, cotangent, window, allowed)
    split_at = reach_blocks * row_count
    remote = jnp.concatenate(
        [key_grads[:split_at].astype(jnp.bfloat16), value_grads[:split_at].astype(jnp.bfloat16)],
        axis=1,
    )
    remote = remote.reshape(reach_blocks, row_count, 2 * half_kv)
    summed = jnp.concatenate([key_grads[split_at:], value_grads[split_at:]], axis=1)
    for offset in range(1, reach_blocks + 1):
        arrived = from_behind(remote[reach_blocks - offset], "seq", -offset)
        summed = summed + arrived.astype(jnp.float32)
    key_total = rotate(summed[:, :half_kv].reshape(row_count, KVH, HD), within, -1.0).reshape(
        row_count, half_kv
    )
    grad_kv = jnp.concatenate([key_total, summed[:, half_kv:]], axis=1).astype(jnp.bfloat16)
    grad_rows = jnp.dot(grad_kv, weight_full.T, preferred_element_type=jnp.float32).astype(
        jnp.bfloat16
    )
    shared = lax.psum_scatter(
        lax.dot_general(
            tokens, grad_kv, (((0,), (0,)), ((), ())), preferred_element_type=jnp.float32
        ).astype(jnp.bfloat16),
        "fsdp",
        scatter_dimension=0,
        tiled=True,
    )
    finished = lax.psum_scatter(shared, "seq", scatter_dimension=1, tiled=True).astype(jnp.float32)
    return (out_rows[None], grad_rows[None], finished)


def solution(mesh):
    in_specs = (
        P("fsdp", "seq", None),
        P("fsdp", "seq", None),
        P("fsdp", None),
        P("fsdp", None),
        P("fsdp", "seq", None),
    )
    out_specs = (P("fsdp", "seq", None), P("fsdp", "seq", None), P("fsdp", "seq"))
    return jax.shard_map(
        on_device, mesh=mesh, in_specs=in_specs, out_specs=out_specs, check_vma=False
    )
```

profile of v0, /device:TPU:4, one launch (start us, length us, event | category | flops | bytes accessed | tf_op | source)
XLA Modules:
  0.0 725.4 jit_solution(4703402251227408415)
XLA Ops:
  11.6 82.5 %all-gather.2.cloned.1.call-done = bf16[2304,2048]{1,0:T(8,128)(2,1)} async-done(((bf16[144,2048]{1,0:T(8,128)(2,1)}), bf16[2304,2048]{1,0:T(8,128)(2,1)}) %all-gather.2.cloned.1.call-update) | async-done | bytes 9437200 | tf_op jit(solution)/shard_map/all_gather | solution.py:123
  94.2 5.1 fusion.32
  100.0 8.5 %collective-permute-start = (bf16[128,2048]{1,0:T(8,128)(2,1)S(1)}, bf16[128,2048]{1,0:T(8,128)(2,1)}, u32[]{:S(2)}, u32[]{:S(2)}) collective-permute-start(bf16[128,2048]{1,0:T(8,128)(2,1)S(1)} %pad_maximum_fusion.1), channel_id=1, source_target_pairs={{0,128},{16,144},{32,160},{48,176},{64,192},{80,208},{96,224},{112... | collective-permute-start | bytes 1572872 | tf_op jit(solution)/shard_map/ppermute | solution.py:19
  108.5 2.7 collective-permute-start.1
  111.2 3.0 collective-permute-start.2
  117.4 1.7 collective-permute-start.6
  120.1 56.2 %collective-permute-start.3 = (bf16[128,2048]{1,0:T(8,128)(2,1)S(1)}, bf16[128,2048]{1,0:T(8,128)(2,1)S(1)}, u32[]{:S(2)}, u32[]{:S(2)}) collective-permute-start(bf16[128,2048]{1,0:T(8,128)(2,1)S(1)} %pad_maximum_fusion.1), channel_id=1, source_target_pairs={{0,80},{16,96},{32,112},{48,128},{64,144},{80,160},{96,176},{112,1... | collective-permute-start | bytes 1572872 | tf_op jit(solution)/shard_map/ppermute | solution.py:19
  176.3 1.9 constant_dynamic-update-slice_fusion.11
  178.2 12.0 %collective-permute-start.4 = (bf16[128,2048]{1,0:T(8,128)(2,1)S(1)}, bf16[128,2048]{1,0:T(8,128)(2,1)S(1)}, u32[]{:S(2)}, u32[]{:S(2)}) collective-permute-start(bf16[128,2048]{1,0:T(8,128)(2,1)S(1)} %pad_maximum_fusion.1), channel_id=1, source_target_pairs={{0,64},{16,80},{32,96},{48,112},{64,128},{80,144},{96,160},{112,17... | collective-permute-start | bytes 1572872 | tf_op jit(solution)/shard_map/ppermute | solution.py:19
  190.2 1.9 constant_dynamic-update-slice_fusion.10
  193.4 1.9 constant_dynamic-update-slice_fusion.9
  196.2 3.1 collective-permute-done.4
  200.1 6.0 collective-permute-done.5
  209.4 6.7 copy.70
  217.0 2.5 broadcast.142.clone
  219.5 2.4 broadcast.142
  221.9 72.9 %while.20 = (s32[]{:T(128)}, bf16[128,2048]{1,0:T(8,128)(2,1)}, f32[1152,1024]{0,1:T(8,128)}, f32[1152,1024]{0,1:T(8,128)}, bf16[1152,2048]{0,1:T(8,128)(2,1)}, ...) while((s32[]{:T(128)}, bf16[128,2048]{1,0:T(8,128)(2,1)}, ...), condition=%wide.region_6.7_spmd.clone, body=%wide.region_4.6_spmd.clone.sunk | while | flops 766655488 | bytes 39024268 | solution.py:109
  222.7 1.9 fusion.82
  224.7 1.4 constant_dynamic-slice_fusion.7
  227.0 1.4 copy-done.1
  230.1 2.2 fusion.85
  232.3 3.1 fusion.87
  235.4 1.4 fusion.86
  236.9 1.6 constant_dynamic-update-slice_fusion.14
  238.4 1.7 constant_dynamic-update-slice_fusion.15
  241.0 1.9 fusion.82
  242.9 1.4 constant_dynamic-slice_fusion.7
  245.2 1.4 copy-done.1
  248.3 2.2 fusion.85
  250.5 3.1 fusion.87
  253.7 1.4 fusion.86
  255.1 1.6 constant_dynamic-update-slice_fusion.14
  256.7 1.7 constant_dynamic-update-slice_fusion.15
  259.2 1.9 fusion.82
  261.1 1.4 constant_dynamic-slice_fusion.7
  263.5 1.4 copy-done.1
  266.5 2.2 fusion.85
  268.7 3.1 fusion.87
  271.9 1.4 fusion.86
  273.3 1.6 constant_dynamic-update-slice_fusion.14
  274.9 1.8 constant_dynamic-update-slice_fusion.15
  277.4 1.9 fusion.82
  281.7 1.4 copy-done.1
  284.8 2.2 fusion.85
  287.0 3.1 fusion.87
  290.1 1.4 fusion.86
  291.6 1.6 constant_dynamic-update-slice_fusion.14
  293.1 1.7 constant_dynamic-update-slice_fusion.15
  294.9 2.5 slice.167
  297.4 2.5 slice.168
  299.9 2.8 fusion.35
  305.3 1.5 collective-permute-start.10
  311.9 47.2 %collective-permute-done.9 = bf16[128,2048]{0,1:T(8,128)(2,1)S(1)} collective-permute-done((bf16[128,2048]{0,1:T(8,128)(2,1)S(1)}, bf16[128,2048]{0,1:T(8,128)(2,1)S(1)}, u32[]{:S(2)}, u32[]{:S(2)}) %collective-permute-start.9) | collective-permute-done | bytes 524320 | tf_op jit(solution)/shard_map/ppermute | solution.py:19
  364.3 62.7 %collective-permute-done.11 = bf16[128,2048]{0,1:T(8,128)(2,1)S(1)} collective-permute-done((bf16[128,2048]{0,1:T(8,128)(2,1)S(1)}, bf16[128,2048]{0,1:T(8,128)(2,1)S(1)}, u32[]{:S(2)}, u32[]{:S(2)}) %collective-permute-start.11) | collective-permute-done | bytes 524320 | tf_op jit(solution)/shard_map/ppermute | solution.py:19
  427.1 13.7 %collective-permute-done.12 = bf16[128,2048]{0,1:T(8,128)(2,1)S(1)} collective-permute-done((bf16[128,2048]{0,1:T(8,128)(2,1)S(1)}, bf16[128,2048]{0,1:T(8,128)(2,1)S(1)}, u32[]{:S(2)}, u32[]{:S(2)}) %collective-permute-start.12) | collective-permute-done | bytes 524320 | tf_op jit(solution)/shard_map/ppermute | solution.py:19
  440.8 46.6 %collective-permute-done.13 = bf16[128,2048]{0,1:T(8,128)(2,1)S(1)} collective-permute-done((bf16[128,2048]{0,1:T(8,128)(2,1)S(1)}, bf16[128,2048]{0,1:T(8,128)(2,1)S(1)}, u32[]{:S(2)}, u32[]{:S(2)}) %collective-permute-start.13) | collective-permute-done | bytes 524320 | tf_op jit(solution)/shard_map/ppermute | solution.py:19
  487.4 1.4 collective-permute-done.14
  490.5 6.5 fusion.22
  497.1 12.7 %copy.97 = bf16[2304,2048]{1,0:T(8,128)(2,1)} copy(bf16[2304,2048]{0,1:T(8,128)(2,1)} %fusion.22) | data formatting | bytes 18874368
  509.9 147.5 %reduce-scatter.7.cloned.1.call-done = bf16[144,2048]{1,0:T(8,128)(2,1)} async-done(((bf16[2304,2048]{1,0:T(8,128)(2,1)}), bf16[144,2048]{1,0:T(8,128)(2,1)}) %reduce-scatter.7.cloned.1.call-update) | async-done | bytes 589840
  657.4 2.2 copy.98
  659.6 7.8 %fusion.23 = bf16[1,128,2304]{2,1,0:T(8,128)(2,1)} fusion(bf16[2304,2048]{1,0:T(8,128)(2,1)} %all-gather.2.cloned.1.call-done, bf16[128,1024]{0,1:T(8,128)(2,1)S(1)} %slice.169, bf16[128,1024]{0,1:T(8,128)(2,1)S(1)} %bitcast.165), kind=kOutput, calls=%fused_computation.55 | convolution fusion | flops 1209303040 | bytes 10551296 | tf_op jit(solution)/shard_map/dot_general | solution.py:161
  667.4 50.0 %reduce-scatter.5.cloned.1.call-done = bf16[144,128]{0,1:T(8,128)(2,1)} async-done(((bf16[144,2048]{0,1:T(8,128)(2,1)}), bf16[144,128]{0,1:T(8,128)(2,1)}) %reduce-scatter.5.cloned.1.call-update) | async-done | bytes 36880 | tf_op jit(solution)/shard_map/reduce_scatter | solution.py:172
  717.3 1.6 copy.75
  (137 shorter events, 45.7 us)
Async XLA Ops:
  7.2 87.0 %copy-start = (bf16[1,128,2304]{2,1,0:T(8,128)(2,1)S(1)}, bf16[1,128,2304]{2,1,0:T(8,128)(2,1)}, u32[]{:S(2)}) copy-start(bf16[1,128,2304]{2,1,0:T(8,128)(2,1)} %param.7) | copy-start | bytes 1769476
  7.2 87.0 %all-gather.2.cloned.1.call-start = ((), (), s32[]{:S(2)}) async-start(), calls=%async_computation.2 | async-start | bytes 10027008 | tf_op jit(solution)/shard_map/all_gather | solution.py:123
  7.9 649.5 %reduce-scatter.7.cloned.1.call-start = ((), (), s32[]{:S(2)}) async-start(), calls=%async_computation.4 | async-start | bytes 10027008
  11.6 87.8 %copy-start.6 = (f32[128,64]{1,0:T(8,128)}, f32[128,64]{1,0:T(8,128)S(1)}, u32[]{:S(2)}) copy-start(f32[128,64]{1,0:T(8,128)S(1)} %get-tuple-element.364) | copy-start | bytes 98308
  99.3 15.5 %copy-start.8 = (bf16[1,128,2048]{2,1,0:T(8,128)(2,1)S(1)}, bf16[1,128,2048]{2,1,0:T(8,128)(2,1)}, u32[]{:S(2)}) copy-start(bf16[1,128,2048]{2,1,0:T(8,128)(2,1)} %param.8) | copy-start | bytes 1572868
  99.3 15.8 %copy-start.9 = (bf16[1,128,2048]{2,1,0:T(8,128)(2,1)S(1)}, bf16[1,128,2048]{2,1,0:T(8,128)(2,1)}, u32[]{:S(2)}) copy-start(bf16[1,128,2048]{2,1,0:T(8,128)(2,1)} %param.11) | copy-start | bytes 1572868
  100.0 20.1 %collective-permute-start = (bf16[128,2048]{1,0:T(8,128)(2,1)S(1)}, bf16[128,2048]{1,0:T(8,128)(2,1)}, u32[]{:S(2)}, u32[]{:S(2)}) collective-permute-start(bf16[128,2048]{1,0:T(8,128)(2,1)S(1)} %pad_maximum_fusion.1), channel_id=1, source_target_pairs={{0,128},{16,144},{32,160},{48,176},{64,192},{80,208},{96,224},{112... | collective-permute-start | bytes 1572872 | tf_op jit(solution)/shard_map/ppermute | solution.py:19
  108.5 69.7 %collective-permute-start.1 = (bf16[128,2048]{1,0:T(8,128)(2,1)S(1)}, bf16[128,2048]{1,0:T(8,128)(2,1)}, u32[]{:S(2)}, u32[]{:S(2)}) collective-permute-start(bf16[128,2048]{1,0:T(8,128)(2,1)S(1)} %pad_maximum_fusion.1), channel_id=1, source_target_pairs={{0,112},{16,128},{32,144},{48,160},{64,176},{80,192},{96,208},{112... | collective-permute-start | bytes 1572872 | tf_op jit(solution)/shard_map/ppermute | solution.py:19
  111.2 80.9 %collective-permute-start.2 = (bf16[128,2048]{1,0:T(8,128)(2,1)S(1)}, bf16[128,2048]{1,0:T(8,128)(2,1)}, u32[]{:S(2)}, u32[]{:S(2)}) collective-permute-start(bf16[128,2048]{1,0:T(8,128)(2,1)S(1)} %pad_maximum_fusion.1), channel_id=1, source_target_pairs={{0,96},{16,112},{32,128},{48,144},{64,160},{80,176},{96,192},{112,... | collective-permute-start | bytes 1572872 | tf_op jit(solution)/shard_map/ppermute | solution.py:19
  116.1 91.7 %collective-permute-start.7 = (bf16[128,2048]{1,0:T(8,128)(2,1)S(1)}, bf16[128,2048]{1,0:T(8,128)(2,1)S(1)}, u32[]{:S(2)}, u32[]{:S(2)}) collective-permute-start(bf16[128,2048]{1,0:T(8,128)(2,1)S(1)} %pad_maximum_fusion.1), channel_id=1, source_target_pairs={{0,16},{16,32},{32,48},{48,64},{64,80},{80,96},{96,112},{112,128},... | collective-permute-start | bytes 1572872 | tf_op jit(solution)/shard_map/ppermute | solution.py:19
  117.4 89.5 %collective-permute-start.6 = (bf16[128,2048]{1,0:T(8,128)(2,1)S(1)}, bf16[128,2048]{1,0:T(8,128)(2,1)S(1)}, u32[]{:S(2)}, u32[]{:S(2)}) collective-permute-start(bf16[128,2048]{1,0:T(8,128)(2,1)S(1)} %pad_maximum_fusion.1), channel_id=1, source_target_pairs={{0,32},{16,48},{32,64},{48,80},{64,96},{80,112},{96,128},{112,144}... | collective-permute-start | bytes 1572872 | tf_op jit(solution)/shard_map/ppermute | solution.py:19
  120.1 75.3 %collective-permute-start.3 = (bf16[128,2048]{1,0:T(8,128)(2,1)S(1)}, bf16[128,2048]{1,0:T(8,128)(2,1)S(1)}, u32[]{:S(2)}, u32[]{:S(2)}) collective-permute-start(bf16[128,2048]{1,0:T(8,128)(2,1)S(1)} %pad_maximum_fusion.1), channel_id=1, source_target_pairs={{0,80},{16,96},{32,112},{48,128},{64,144},{80,160},{96,176},{112,1... | collective-permute-start | bytes 1572872 | tf_op jit(solution)/shard_map/ppermute | solution.py:19
  178.2 21.1 %collective-permute-start.4 = (bf16[128,2048]{1,0:T(8,128)(2,1)S(1)}, bf16[128,2048]{1,0:T(8,128)(2,1)S(1)}, u32[]{:S(2)}, u32[]{:S(2)}) collective-permute-start(bf16[128,2048]{1,0:T(8,128)(2,1)S(1)} %pad_maximum_fusion.1), channel_id=1, source_target_pairs={{0,64},{16,80},{32,96},{48,112},{64,128},{80,144},{96,160},{112,17... | collective-permute-start | bytes 1572872 | tf_op jit(solution)/shard_map/ppermute | solution.py:19
  192.1 14.0 %collective-permute-start.5 = (bf16[128,2048]{1,0:T(8,128)(2,1)S(1)}, bf16[128,2048]{1,0:T(8,128)(2,1)S(1)}, u32[]{:S(2)}, u32[]{:S(2)}) collective-permute-start(bf16[128,2048]{1,0:T(8,128)(2,1)S(1)} %pad_maximum_fusion.1), channel_id=1, source_target_pairs={{0,48},{16,64},{32,80},{48,96},{64,112},{80,128},{96,144},{112,160... | collective-permute-start | bytes 1572872 | tf_op jit(solution)/shard_map/ppermute | solution.py:19
  221.9 0.8 copy-start.4
  222.0 5.0 copy-start.3
  224.7 4.3 copy-start.2
  227.0 1.5 copy-start.1
  227.0 1.5 copy-start.11
  235.4 4.8 copy-start.5
  240.2 0.8 copy-start.4
  240.2 5.1 copy-start.3
  242.9 4.3 copy-start.2
  245.2 1.5 copy-start.1
  245.2 1.5 copy-start.11
  253.6 4.7 copy-start.5
  258.4 0.8 copy-start.4
  258.4 5.0 copy-start.3
  261.1 4.3 copy-start.2
  263.4 1.5 copy-start.1
  263.4 1.5 copy-start.11
  271.9 4.8 copy-start.5
  276.6 0.8 copy-start.4
  276.7 5.0 copy-start.3
  279.4 4.3 copy-start.2
  281.7 1.5 copy-start.1
  281.7 1.5 copy-start.11
  290.1 4.8 copy-start.5
  302.7 7.9 %collective-permute-start.8 = (bf16[128,2048]{0,1:T(8,128)(2,1)S(1)}, bf16[128,2048]{0,1:T(8,128)(2,1)S(1)}, u32[]{:S(2)}, u32[]{:S(2)}) collective-permute-start(bf16[128,2048]{0,1:T(8,128)(2,1)S(1)} %get-tuple-element.348), channel_id=1, source_target_pairs={{16,0},{32,16},{48,32},{64,48},{80,64},{96,80},{112,96},{128,112},... | collective-permute-start | bytes 1572872 | tf_op jit(solution)/shard_map/ppermute | solution.py:19
  304.0 55.1 %collective-permute-start.9 = (bf16[128,2048]{0,1:T(8,128)(2,1)S(1)}, bf16[128,2048]{0,1:T(8,128)(2,1)S(1)}, u32[]{:S(2)}, u32[]{:S(2)}) collective-permute-start(bf16[128,2048]{0,1:T(8,128)(2,1)S(1)} %get-tuple-element.349), channel_id=1, source_target_pairs={{32,0},{48,16},{64,32},{80,48},{96,64},{112,80},{128,96},{144,112}... | collective-permute-start | bytes 1572872 | tf_op jit(solution)/shard_map/ppermute | solution.py:19
  305.3 55.6 %collective-permute-start.10 = (bf16[128,2048]{0,1:T(8,128)(2,1)S(1)}, bf16[128,2048]{0,1:T(8,128)(2,1)S(1)}, u32[]{:S(2)}, u32[]{:S(2)}) collective-permute-start(bf16[128,2048]{0,1:T(8,128)(2,1)S(1)} %get-tuple-element.350), channel_id=1, source_target_pairs={{48,0},{64,16},{80,32},{96,48},{112,64},{128,80},{144,96},{160,112... | collective-permute-start | bytes 1572872 | tf_op jit(solution)/shard_map/ppermute | solution.py:19
  306.7 120.3 %collective-permute-start.11 = (bf16[128,2048]{0,1:T(8,128)(2,1)S(1)}, bf16[128,2048]{0,1:T(8,128)(2,1)S(1)}, u32[]{:S(2)}, u32[]{:S(2)}) collective-permute-start(bf16[128,2048]{0,1:T(8,128)(2,1)S(1)} %get-tuple-element.351), channel_id=1, source_target_pairs={{64,0},{80,16},{96,32},{112,48},{128,64},{144,80},{160,96},{176,11... | collective-permute-start | bytes 1572872 | tf_op jit(solution)/shard_map/ppermute | solution.py:19
  308.0 132.7 %collective-permute-start.12 = (bf16[128,2048]{0,1:T(8,128)(2,1)S(1)}, bf16[128,2048]{0,1:T(8,128)(2,1)S(1)}, u32[]{:S(2)}, u32[]{:S(2)}) collective-permute-start(bf16[128,2048]{0,1:T(8,128)(2,1)S(1)} %get-tuple-element.352), channel_id=1, source_target_pairs={{80,0},{96,16},{112,32},{128,48},{144,64},{160,80},{176,96},{192,1... | collective-permute-start | bytes 1572872 | tf_op jit(solution)/shard_map/ppermute | solution.py:19
  310.6 176.8 %collective-permute-start.13 = (bf16[128,2048]{0,1:T(8,128)(2,1)S(1)}, bf16[128,2048]{0,1:T(8,128)(2,1)S(1)}, u32[]{:S(2)}, u32[]{:S(2)}) collective-permute-start(bf16[128,2048]{0,1:T(8,128)(2,1)S(1)} %get-tuple-element.353), channel_id=1, source_target_pairs={{96,0},{112,16},{128,32},{144,48},{160,64},{176,80},{192,96},{208,... | collective-permute-start | bytes 1572872 | tf_op jit(solution)/shard_map/ppermute | solution.py:19
  359.1 128.3 %collective-permute-start.15 = (bf16[128,2048]{0,1:T(8,128)(2,1)S(1)}, bf16[128,2048]{0,1:T(8,128)(2,1)S(1)}, u32[]{:S(2)}, u32[]{:S(2)}) collective-permute-start(bf16[128,2048]{0,1:T(8,128)(2,1)S(1)} %get-tuple-element.354), channel_id=1, source_target_pairs={{128,0},{144,16},{160,32},{176,48},{192,64},{208,80},{224,96},{240... | collective-permute-start | bytes 1572872 | tf_op jit(solution)/shard_map/ppermute | solution.py:19
  360.9 128.0 %collective-permute-start.14 = (bf16[128,2048]{0,1:T(8,128)(2,1)S(1)}, bf16[128,2048]{0,1:T(8,128)(2,1)S(1)}, u32[]{:S(2)}, u32[]{:S(2)}) collective-permute-start(bf16[128,2048]{0,1:T(8,128)(2,1)S(1)} %get-tuple-element.355), channel_id=1, source_target_pairs={{112,0},{128,16},{144,32},{160,48},{176,64},{192,80},{208,96},{224... | collective-permute-start | bytes 1572872 | tf_op jit(solution)/shard_map/ppermute | solution.py:19
  364.3 125.7 %copy-start.7 = (f32[128,64]{1,0:T(8,128)S(1)}, f32[128,64]{1,0:T(8,128)}, u32[]{:S(2)}) copy-start(f32[128,64]{1,0:T(8,128)} %copy-done.6) | copy-start | bytes 98308
  364.3 125.7 %copy-start.10 = (f32[128,64]{1,0:T(8,128)S(1)}, f32[128,64]{1,0:T(8,128)}, u32[]{:S(2)}) copy-start(f32[128,64]{1,0:T(8,128)} %get-tuple-element.362) | copy-start | bytes 98308
  509.8 207.5 %reduce-scatter.5.cloned.1.call-start = ((), (), s32[]{:S(2)}) async-start(), calls=%async_computation.3 | async-start | bytes 1114112 | tf_op jit(solution)/shard_map/reduce_scatter | solution.py:172
Sparse Core Ops, SparseCore 0:
  10.5 83.6 all-gather.1
  509.9 147.4 reduce-scatter.6
  660.1 57.2 reduce-scatter.4
where the time goes:
time: 727 us; the launch traced here: 725 us
  waiting for transfers between devices  464 us (64%)
  starting transfers between devices  97.3 us (13%)
  local copies, waits for them, and re-layouts  79.2 us (11%)
  matrix products  42.6 us (6%)
  other arithmetic  27.7 us (4%)
  between operations  14.1 us (2%)
    ppermute x16, waiting for transfers between devices, from_behind(): lax.ppermute(value, axis, [(source, source + steps) for source in range(f...  183 us
    unnamed x4, waiting for transfers between devices  148 us
    ppermute x16, starting transfers between devices, from_behind(): lax.ppermute(value, axis, [(source, source + steps) for source in range(f...  97.2 us
    all_gather x1, waiting for transfers between devices, on_device(): weight_full = lax.all_gather(w_kv, 'fsdp', axis=0, tiled=True)  82.5 us
    reduce_scatter x1, waiting for transfers between devices, on_device(): lax.psum_scatter(shared, 'seq', scatter_dimension=1, tiled=True)  50 us
    unnamed x31, local copies, waits for them, and re-layouts  35 us
  transfers between devices with their start and end apart: 19, of which 13 were waited for; matrix products, arithmetic and copies ran while one was open for 3% of the time, Pallas kernels for 0%

commit v1 on v0

--- a/solution.py
+++ b/solution.py
@@ -120,7 +120,9 @@
     shard_index = lax.axis_index("seq")
     reach_blocks = min((WIN + row_count - 2) // row_count, seq_count - 1)
     half_kv = KVH * HD
-    weight_full = lax.all_gather(w_kv, "fsdp", axis=0, tiled=True)
+    weight_full = jnp.concatenate(
+        lax.all_to_all(jnp.stack([w_kv] * lax.axis_size("fsdp")), "fsdp", 0, 0), axis=0
+    )
     projected = jnp.dot(tokens, weight_full, preferred_element_type=jnp.float32)
     places = shard_index * row_count + jnp.arange(row_count, dtype=jnp.int32)
     doc_index, within = doc_layout(lengths, places)

time: 727 us -> 826 us (1.14)
  waiting for transfers between devices: 464 us -> 549 us
    all_to_all x0 -> x1, waiting for transfers between devices: none -> 145 us  [on_device(): lax.all_to_all(jnp.stack([w_kv] * lax.axis_size('fsdp')), 'fsdp', 0, 0)]
    all_gather x1 -> x0, waiting for transfers between devices: 82.5 us -> none  [on_device(): weight_full = lax.all_gather(w_kv, 'fsdp', axis=0, tiled=True)]
    unnamed x4 -> x3, waiting for transfers between devices: 148 us -> 171 us
    unnamed x31 -> x33, local copies, waits for them, and re-layouts: 35 us -> 35 us
where the time goes in v1:
time: 826 us; the launch traced here: 824 us
  waiting for transfers between devices  549 us (66%)
  starting transfers between devices  105 us (13%)
  local copies, waits for them, and re-layouts  85.2 us (10%)
  matrix products  42.5 us (5%)
  other arithmetic  27 us (3%)
  between operations  14.4 us (2%)
    ppermute x16, waiting for transfers between devices, from_behind(): lax.ppermute(value, axis, [(source, source + steps) for source in range(f...  183 us
    unnamed x3, waiting for transfers between devices  171 us
    all_to_all x1, waiting for transfers between devices, on_device(): lax.all_to_all(jnp.stack([w_kv] * lax.axis_size('fsdp')), 'fsdp', 0, 0)  145 us
    ppermute x16, starting transfers between devices, from_behind(): lax.ppermute(value, axis, [(source, source + steps) for source in range(f...  97.4 us
    reduce_scatter x1, waiting for transfers between devices, on_device(): lax.psum_scatter(shared, 'seq', scatter_dimension=1, tiled=True)  49.9 us
    unnamed x33, local copies, waits for them, and re-layouts  35 us
  transfers between devices with their start and end apart: 19, of which 13 were waited for; matrix products, arithmetic and copies ran while one was open for 3% of the time, Pallas kernels for 0%

profile of v1, /device:TPU:4, one launch (start us, length us, event | category | flops | bytes accessed | tf_op | source)
XLA Modules:
  0.0 823.9 jit_solution(10230815314534987338)
XLA Ops:
  7.2 6.0 stack.2
  13.2 7.6 all-to-all-start
  23.8 145.5 %all-to-all-done = bf16[16,144,2048]{2,1,0:T(8,128)(2,1)} async-done(((bf16[16,144,2048]{2,1,0:T(8,128)(2,1)}), bf16[16,144,2048]{2,1,0:T(8,128)(2,1)}, u32[]{:S(2)}, u32[]{:S(2)}) %all-to-all-start) | async-done | bytes 9437216 | tf_op jit(solution)/shard_map/all_to_all | solution.py:124
  169.3 5.1 fusion.32
  175.1 9.9 %collective-permute-start = (bf16[128,2048]{1,0:T(8,128)(2,1)S(1)}, bf16[128,2048]{1,0:T(8,128)(2,1)}, u32[]{:S(2)}, u32[]{:S(2)}) collective-permute-start(bf16[128,2048]{1,0:T(8,128)(2,1)S(1)} %pad_maximum_fusion.1), channel_id=1, source_target_pairs={{0,128},{16,144},{32,160},{48,176},{64,192},{80,208},{96,224},{112... | collective-permute-start | bytes 1572872 | tf_op jit(solution)/shard_map/ppermute | solution.py:19
  185.0 2.1 collective-permute-start.1
  187.2 4.6 collective-permute-start.2
  196.7 54.4 %collective-permute-start.3 = (bf16[128,2048]{1,0:T(8,128)(2,1)S(1)}, bf16[128,2048]{1,0:T(8,128)(2,1)S(1)}, u32[]{:S(2)}, u32[]{:S(2)}) collective-permute-start(bf16[128,2048]{1,0:T(8,128)(2,1)S(1)} %pad_maximum_fusion.1), channel_id=1, source_target_pairs={{0,80},{16,96},{32,112},{48,128},{64,144},{80,160},{96,176},{112,1... | collective-permute-start | bytes 1572872 | tf_op jit(solution)/shard_map/ppermute | solution.py:19
  251.2 1.9 constant_dynamic-update-slice_fusion.11
  253.1 11.7 %collective-permute-start.4 = (bf16[128,2048]{1,0:T(8,128)(2,1)S(1)}, bf16[128,2048]{1,0:T(8,128)(2,1)S(1)}, u32[]{:S(2)}, u32[]{:S(2)}) collective-permute-start(bf16[128,2048]{1,0:T(8,128)(2,1)S(1)} %pad_maximum_fusion.1), channel_id=1, source_target_pairs={{0,64},{16,80},{32,96},{48,112},{64,128},{80,144},{96,160},{112,17... | collective-permute-start | bytes 1572872 | tf_op jit(solution)/shard_map/ppermute | solution.py:19
  264.8 1.9 constant_dynamic-update-slice_fusion.10
  266.7 1.5 collective-permute-start.5
  268.2 1.9 constant_dynamic-update-slice_fusion.9
  270.9 3.3 collective-permute-done.4
  275.0 5.3 collective-permute-done.5
  283.7 6.7 copy.70
  291.3 2.5 broadcast.144.clone
  293.8 2.4 broadcast.144
  296.2 72.9 %while.20 = (s32[]{:T(128)}, bf16[128,2048]{1,0:T(8,128)(2,1)}, f32[1152,1024]{0,1:T(8,128)}, f32[1152,1024]{0,1:T(8,128)}, bf16[1152,2048]{0,1:T(8,128)(2,1)}, ...) while((s32[]{:T(128)}, bf16[128,2048]{1,0:T(8,128)(2,1)}, ...), condition=%wide.region_6.7_spmd.clone, body=%wide.region_4.6_spmd.clone.sunk | while | flops 766655488 | bytes 39024268 | solution.py:109
  297.0 1.9 fusion.82
  301.3 1.4 copy-done.1
  304.4 2.2 fusion.85
  306.5 3.1 fusion.87
  309.7 1.4 fusion.86
  311.1 1.6 constant_dynamic-update-slice_fusion.14
  312.7 1.7 constant_dynamic-update-slice_fusion.15
  315.2 1.9 fusion.82
  319.5 1.4 copy-done.1
  322.6 2.2 fusion.85
  324.8 3.1 fusion.87
  327.9 1.4 fusion.86
  329.4 1.6 constant_dynamic-update-slice_fusion.14
  330.9 1.7 constant_dynamic-update-slice_fusion.15
  333.5 1.9 fusion.82
  337.7 1.4 copy-done.1
  340.8 2.2 fusion.85
  343.0 3.1 fusion.87
  346.1 1.4 fusion.86
  347.6 1.6 constant_dynamic-update-slice_fusion.14
  349.2 1.8 constant_dynamic-update-slice_fusion.15
  351.7 1.9 fusion.82
  356.0 1.4 copy-done.1
  359.1 2.2 fusion.85
  361.2 3.1 fusion.87
  364.4 1.4 fusion.86
  365.8 1.6 constant_dynamic-update-slice_fusion.14
  367.4 1.7 constant_dynamic-update-slice_fusion.15
  369.1 2.5 slice.167
  371.6 2.5 slice.168
  374.2 2.8 fusion.35
  383.4 2.0 collective-permute-done.8
  386.8 46.3 %collective-permute-done.9 = bf16[128,2048]{0,1:T(8,128)(2,1)S(1)} collective-permute-done((bf16[128,2048]{0,1:T(8,128)(2,1)S(1)}, bf16[128,2048]{0,1:T(8,128)(2,1)S(1)}, u32[]{:S(2)}, u32[]{:S(2)}) %collective-permute-start.9) | collective-permute-done | bytes 524320 | tf_op jit(solution)/shard_map/ppermute | solution.py:19
  434.9 1.5 collective-permute-start.14
  438.6 62.6 %collective-permute-done.11 = bf16[128,2048]{0,1:T(8,128)(2,1)S(1)} collective-permute-done((bf16[128,2048]{0,1:T(8,128)(2,1)S(1)}, bf16[128,2048]{0,1:T(8,128)(2,1)S(1)}, u32[]{:S(2)}, u32[]{:S(2)}) %collective-permute-start.11) | collective-permute-done | bytes 524320 | tf_op jit(solution)/shard_map/ppermute | solution.py:19
  501.2 13.8 %collective-permute-done.12 = bf16[128,2048]{0,1:T(8,128)(2,1)S(1)} collective-permute-done((bf16[128,2048]{0,1:T(8,128)(2,1)S(1)}, bf16[128,2048]{0,1:T(8,128)(2,1)S(1)}, u32[]{:S(2)}, u32[]{:S(2)}) %collective-permute-start.12) | collective-permute-done | bytes 524320 | tf_op jit(solution)/shard_map/ppermute | solution.py:19
  515.0 47.1 %collective-permute-done.13 = bf16[128,2048]{0,1:T(8,128)(2,1)S(1)} collective-permute-done((bf16[128,2048]{0,1:T(8,128)(2,1)S(1)}, bf16[128,2048]{0,1:T(8,128)(2,1)S(1)}, u32[]{:S(2)}, u32[]{:S(2)}) %collective-permute-start.13) | collective-permute-done | bytes 524320 | tf_op jit(solution)/shard_map/ppermute | solution.py:19
  562.1 1.4 collective-permute-done.14
  565.2 6.5 fusion.22
  571.8 12.7 %copy.97 = bf16[2304,2048]{1,0:T(8,128)(2,1)} copy(bf16[2304,2048]{0,1:T(8,128)(2,1)} %fusion.22) | data formatting | bytes 18874368
  584.5 171.0 %reduce-scatter.7.cloned.1.call-done = bf16[144,2048]{1,0:T(8,128)(2,1)} async-done(((bf16[2304,2048]{1,0:T(8,128)(2,1)}), bf16[144,2048]{1,0:T(8,128)(2,1)}) %reduce-scatter.7.cloned.1.call-update) | async-done | bytes 589840
  755.6 2.2 copy.98
  757.8 7.8 fusion.23
  765.6 49.9 %reduce-scatter.5.cloned.1.call-done = bf16[144,128]{0,1:T(8,128)(2,1)} async-done(((bf16[144,2048]{0,1:T(8,128)(2,1)}), bf16[144,128]{0,1:T(8,128)(2,1)}) %reduce-scatter.5.cloned.1.call-update) | async-done | bytes 36880 | tf_op jit(solution)/shard_map/reduce_scatter | solution.py:174
  815.5 1.6 copy.75
  (139 shorter events, 46.7 us)
Async XLA Ops:
  7.2 162.1 %copy-start = (bf16[1,128,2304]{2,1,0:T(8,128)(2,1)S(1)}, bf16[1,128,2304]{2,1,0:T(8,128)(2,1)}, u32[]{:S(2)}) copy-start(bf16[1,128,2304]{2,1,0:T(8,128)(2,1)} %param.7) | copy-start | bytes 1769476
  13.1 7.6 copy-start.12
  13.2 156.2 %all-to-all-start = ((bf16[16,144,2048]{2,1,0:T(8,128)(2,1)}), bf16[16,144,2048]{2,1,0:T(8,128)(2,1)}, u32[]{:S(2)}, u32[]{:S(2)}) async-start(bf16[16,144,2048]{2,1,0:T(8,128)(2,1)} %stack.2), calls=%async_computation | async-start | bytes 18874368 | tf_op jit(solution)/shard_map/all_to_all | solution.py:124
  20.7 734.9 %reduce-scatter.7.cloned.1.call-start = ((), (), s32[]{:S(2)}) async-start(), calls=%async_computation.4 | async-start | bytes 10027008
  23.8 150.8 %copy-start.6 = (f32[128,64]{1,0:T(8,128)}, f32[128,64]{1,0:T(8,128)S(1)}, u32[]{:S(2)}) copy-start(f32[128,64]{1,0:T(8,128)S(1)} %get-tuple-element.364) | copy-start | bytes 98308
  174.4 18.1 %copy-start.8 = (bf16[1,128,2048]{2,1,0:T(8,128)(2,1)S(1)}, bf16[1,128,2048]{2,1,0:T(8,128)(2,1)}, u32[]{:S(2)}) copy-start(bf16[1,128,2048]{2,1,0:T(8,128)(2,1)} %param.8) | copy-start | bytes 1572868
  174.4 18.3 %copy-start.9 = (bf16[1,128,2048]{2,1,0:T(8,128)(2,1)S(1)}, bf16[1,128,2048]{2,1,0:T(8,128)(2,1)}, u32[]{:S(2)}) copy-start(bf16[1,128,2048]{2,1,0:T(8,128)(2,1)} %param.11) | copy-start | bytes 1572868
  175.1 21.6 %collective-permute-start = (bf16[128,2048]{1,0:T(8,128)(2,1)S(1)}, bf16[128,2048]{1,0:T(8,128)(2,1)}, u32[]{:S(2)}, u32[]{:S(2)}) collective-permute-start(bf16[128,2048]{1,0:T(8,128)(2,1)S(1)} %pad_maximum_fusion.1), channel_id=1, source_target_pairs={{0,128},{16,144},{32,160},{48,176},{64,192},{80,208},{96,224},{112... | collective-permute-start | bytes 1572872 | tf_op jit(solution)/shard_map/ppermute | solution.py:19
  185.0 68.1 %collective-permute-start.1 = (bf16[128,2048]{1,0:T(8,128)(2,1)S(1)}, bf16[128,2048]{1,0:T(8,128)(2,1)}, u32[]{:S(2)}, u32[]{:S(2)}) collective-permute-start(bf16[128,2048]{1,0:T(8,128)(2,1)S(1)} %pad_maximum_fusion.1), channel_id=1, source_target_pairs={{0,112},{16,128},{32,144},{48,160},{64,176},{80,192},{96,208},{112... | collective-permute-start | bytes 1572872 | tf_op jit(solution)/shard_map/ppermute | solution.py:19
  187.2 79.4 %collective-permute-start.2 = (bf16[128,2048]{1,0:T(8,128)(2,1)S(1)}, bf16[128,2048]{1,0:T(8,128)(2,1)}, u32[]{:S(2)}, u32[]{:S(2)}) collective-permute-start(bf16[128,2048]{1,0:T(8,128)(2,1)S(1)} %pad_maximum_fusion.1), channel_id=1, source_target_pairs={{0,96},{16,112},{32,128},{48,144},{64,160},{80,176},{96,192},{112,... | collective-permute-start | bytes 1572872 | tf_op jit(solution)/shard_map/ppermute | solution.py:19
  193.8 88.3 %collective-permute-start.7 = (bf16[128,2048]{1,0:T(8,128)(2,1)S(1)}, bf16[128,2048]{1,0:T(8,128)(2,1)S(1)}, u32[]{:S(2)}, u32[]{:S(2)}) collective-permute-start(bf16[128,2048]{1,0:T(8,128)(2,1)S(1)} %pad_maximum_fusion.1), channel_id=1, source_target_pairs={{0,16},{16,32},{32,48},{48,64},{64,80},{80,96},{96,112},{112,128},... | collective-permute-start | bytes 1572872 | tf_op jit(solution)/shard_map/ppermute | solution.py:19
  195.1 86.1 %collective-permute-start.6 = (bf16[128,2048]{1,0:T(8,128)(2,1)S(1)}, bf16[128,2048]{1,0:T(8,128)(2,1)S(1)}, u32[]{:S(2)}, u32[]{:S(2)}) collective-permute-start(bf16[128,2048]{1,0:T(8,128)(2,1)S(1)} %pad_maximum_fusion.1), channel_id=1, source_target_pairs={{0,32},{16,48},{32,64},{48,80},{64,96},{80,112},{96,128},{112,144}... | collective-permute-start | bytes 1572872 | tf_op jit(solution)/shard_map/ppermute | solution.py:19
  196.7 73.3 %collective-permute-start.3 = (bf16[128,2048]{1,0:T(8,128)(2,1)S(1)}, bf16[128,2048]{1,0:T(8,128)(2,1)S(1)}, u32[]{:S(2)}, u32[]{:S(2)}) collective-permute-start(bf16[128,2048]{1,0:T(8,128)(2,1)S(1)} %pad_maximum_fusion.1), channel_id=1, source_target_pairs={{0,80},{16,96},{32,112},{48,128},{64,144},{80,160},{96,176},{112,1... | collective-permute-start | bytes 1572872 | tf_op jit(solution)/shard_map/ppermute | solution.py:19
  253.1 21.1 %collective-permute-start.4 = (bf16[128,2048]{1,0:T(8,128)(2,1)S(1)}, bf16[128,2048]{1,0:T(8,128)(2,1)S(1)}, u32[]{:S(2)}, u32[]{:S(2)}) collective-permute-start(bf16[128,2048]{1,0:T(8,128)(2,1)S(1)} %pad_maximum_fusion.1), channel_id=1, source_target_pairs={{0,64},{16,80},{32,96},{48,112},{64,128},{80,144},{96,160},{112,17... | collective-permute-start | bytes 1572872 | tf_op jit(solution)/shard_map/ppermute | solution.py:19
  266.7 13.7 %collective-permute-start.5 = (bf16[128,2048]{1,0:T(8,128)(2,1)S(1)}, bf16[128,2048]{1,0:T(8,128)(2,1)S(1)}, u32[]{:S(2)}, u32[]{:S(2)}) collective-permute-start(bf16[128,2048]{1,0:T(8,128)(2,1)S(1)} %pad_maximum_fusion.1), channel_id=1, source_target_pairs={{0,48},{16,64},{32,80},{48,96},{64,112},{80,128},{96,144},{112,160... | collective-permute-start | bytes 1572872 | tf_op jit(solution)/shard_map/ppermute | solution.py:19
  296.2 0.8 copy-start.4
  296.2 5.0 copy-start.3
  299.0 4.3 copy-start.2
  301.2 1.5 copy-start.1
  301.3 1.5 copy-start.11
  309.7 4.8 copy-start.5
  314.4 0.8 copy-start.4
  314.5 5.1 copy-start.3
  317.2 4.3 copy-start.2
  319.5 1.5 copy-start.1
  319.5 1.5 copy-start.11
  327.9 4.7 copy-start.5
  332.7 0.8 copy-start.4
  332.7 5.0 copy-start.3
  335.4 4.3 copy-start.2
  337.7 1.5 copy-start.1
  337.7 1.5 copy-start.11
  346.1 4.8 copy-start.5
  350.9 0.8 copy-start.4
  350.9 5.0 copy-start.3
  353.7 4.3 copy-start.2
  356.0 1.5 copy-start.1
  356.0 1.5 copy-start.11
  364.4 4.8 copy-start.5
  376.9 8.5 %collective-permute-start.8 = (bf16[128,2048]{0,1:T(8,128)(2,1)S(1)}, bf16[128,2048]{0,1:T(8,128)(2,1)S(1)}, u32[]{:S(2)}, u32[]{:S(2)}) collective-permute-start(bf16[128,2048]{0,1:T(8,128)(2,1)S(1)} %get-tuple-element.348), channel_id=1, source_target_pairs={{16,0},{32,16},{48,32},{64,48},{80,64},{96,80},{112,96},{128,112},... | collective-permute-start | bytes 1572872 | tf_op jit(solution)/shard_map/ppermute | solution.py:19
  378.2 54.9 %collective-permute-start.9 = (bf16[128,2048]{0,1:T(8,128)(2,1)S(1)}, bf16[128,2048]{0,1:T(8,128)(2,1)S(1)}, u32[]{:S(2)}, u32[]{:S(2)}) collective-permute-start(bf16[128,2048]{0,1:T(8,128)(2,1)S(1)} %get-tuple-element.349), channel_id=1, source_target_pairs={{32,0},{48,16},{64,32},{80,48},{96,64},{112,80},{128,96},{144,112}... | collective-permute-start | bytes 1572872 | tf_op jit(solution)/shard_map/ppermute | solution.py:19
  379.5 55.4 %collective-permute-start.10 = (bf16[128,2048]{0,1:T(8,128)(2,1)S(1)}, bf16[128,2048]{0,1:T(8,128)(2,1)S(1)}, u32[]{:S(2)}, u32[]{:S(2)}) collective-permute-start(bf16[128,2048]{0,1:T(8,128)(2,1)S(1)} %get-tuple-element.350), channel_id=1, source_target_pairs={{48,0},{64,16},{80,32},{96,48},{112,64},{128,80},{144,96},{160,112... | collective-permute-start | bytes 1572872 | tf_op jit(solution)/shard_map/ppermute | solution.py:19
  380.8 120.4 %collective-permute-start.11 = (bf16[128,2048]{0,1:T(8,128)(2,1)S(1)}, bf16[128,2048]{0,1:T(8,128)(2,1)S(1)}, u32[]{:S(2)}, u32[]{:S(2)}) collective-permute-start(bf16[128,2048]{0,1:T(8,128)(2,1)S(1)} %get-tuple-element.351), channel_id=1, source_target_pairs={{64,0},{80,16},{96,32},{112,48},{128,64},{144,80},{160,96},{176,11... | collective-permute-start | bytes 1572872 | tf_op jit(solution)/shard_map/ppermute | solution.py:19
  382.1 132.9 %collective-permute-start.12 = (bf16[128,2048]{0,1:T(8,128)(2,1)S(1)}, bf16[128,2048]{0,1:T(8,128)(2,1)S(1)}, u32[]{:S(2)}, u32[]{:S(2)}) collective-permute-start(bf16[128,2048]{0,1:T(8,128)(2,1)S(1)} %get-tuple-element.352), channel_id=1, source_target_pairs={{80,0},{96,16},{112,32},{128,48},{144,64},{160,80},{176,96},{192,1... | collective-permute-start | bytes 1572872 | tf_op jit(solution)/shard_map/ppermute | solution.py:19
  385.5 176.6 %collective-permute-start.13 = (bf16[128,2048]{0,1:T(8,128)(2,1)S(1)}, bf16[128,2048]{0,1:T(8,128)(2,1)S(1)}, u32[]{:S(2)}, u32[]{:S(2)}) collective-permute-start(bf16[128,2048]{0,1:T(8,128)(2,1)S(1)} %get-tuple-element.353), channel_id=1, source_target_pairs={{96,0},{112,16},{128,32},{144,48},{160,64},{176,80},{192,96},{208,... | collective-permute-start | bytes 1572872 | tf_op jit(solution)/shard_map/ppermute | solution.py:19
  433.1 129.0 %collective-permute-start.15 = (bf16[128,2048]{0,1:T(8,128)(2,1)S(1)}, bf16[128,2048]{0,1:T(8,128)(2,1)S(1)}, u32[]{:S(2)}, u32[]{:S(2)}) collective-permute-start(bf16[128,2048]{0,1:T(8,128)(2,1)S(1)} %get-tuple-element.354), channel_id=1, source_target_pairs={{128,0},{144,16},{160,32},{176,48},{192,64},{208,80},{224,96},{240... | collective-permute-start | bytes 1572872 | tf_op jit(solution)/shard_map/ppermute | solution.py:19
  434.9 128.6 %collective-permute-start.14 = (bf16[128,2048]{0,1:T(8,128)(2,1)S(1)}, bf16[128,2048]{0,1:T(8,128)(2,1)S(1)}, u32[]{:S(2)}, u32[]{:S(2)}) collective-permute-start(bf16[128,2048]{0,1:T(8,128)(2,1)S(1)} %get-tuple-element.355), channel_id=1, source_target_pairs={{112,0},{128,16},{144,32},{160,48},{176,64},{192,80},{208,96},{224... | collective-permute-start | bytes 1572872 | tf_op jit(solution)/shard_map/ppermute | solution.py:19
  438.6 126.1 %copy-start.7 = (f32[128,64]{1,0:T(8,128)S(1)}, f32[128,64]{1,0:T(8,128)}, u32[]{:S(2)}) copy-start(f32[128,64]{1,0:T(8,128)} %copy-done.6) | copy-start | bytes 98308
  438.6 126.1 %copy-start.10 = (f32[128,64]{1,0:T(8,128)S(1)}, f32[128,64]{1,0:T(8,128)}, u32[]{:S(2)}) copy-start(f32[128,64]{1,0:T(8,128)} %get-tuple-element.362) | copy-start | bytes 98308
  584.5 231.0 %reduce-scatter.5.cloned.1.call-start = ((), (), s32[]{:S(2)}) async-start(), calls=%async_computation.3 | async-start | bytes 1114112 | tf_op jit(solution)/shard_map/reduce_scatter | solution.py:174
Sparse Core Ops, SparseCore 0:
  584.6 170.9 reduce-scatter.6
  758.3 57.2 reduce-scatter.4
